TPU v7x, 256 devices: a whole 4x4x8 slice. The times are simulated.
256 devices in a mesh: ctx: 16 (over z_hi, y), head: 16 (over x, z_lo, core).
Axes of the slice: x: 4, y: 4, z: 8 (z_hi: 4, z_lo: 2; z = z_hi * 2 + z_lo), core: 2. Of those that a mesh axis runs over, the one named last changes fastest.
Arguments:
- queries: bfloat16 [4096, 16384], P('ctx', 'head'), may hold values from -10 to 10
- key_states: bfloat16 [4096, 1024], P('ctx'), may hold values from -10 to 10
- value_states: bfloat16 [4096, 1024], P('ctx'), may hold values from -6 to 6
- vertical_blocks: int32 [128, 4], P('head'), may hold values from 0 to 31, as said below
- slash_offsets: int32 [128, 4], P('head'), may hold values from 0 to 31, as said below
- positions: int32 [4096], P('ctx'), may hold values from 0 to 32767, as said below
- out_weight: bfloat16 [16384, 16384], P('head', 'ctx'), may hold values from -0.25 to 0.25
Outputs:
- projected: bfloat16 [4096, 16384], P('head', 'ctx')
Inputs may be any that keep to these rules, and one draw needn't show every extreme that they name: `vertical_blocks`: each head's 4 vertical blocks are distinct. `slash_offsets`: each head's 4 offsets are distinct and the first of them is 0. `positions`: positions rise by one inside each block of 128 tokens; block b starts at a multiple of 128 at or after b * 1024 and before (b + 1) * 1024.
All inputs are finite; a program needn't handle non-finite values.
Results may differ from a plain program's by a relative error of at most 0.025.
Values may be sent and summed in bfloat16 or wider, within the bound.
A program may use at most 64 MiB of HBM per device.

v0:
```python
import math
import jax
import jax.numpy as jnp
from jax import lax
from jax.sharding import PartitionSpec as P

HD = 128
GROUP = 16
BLK = 128


def rotate_heads(states, positions):
    half_width = states.shape[-1] // 2
    exponents = jnp.arange(half_width, dtype=jnp.float32) * (2.0 / states.shape[-1])
    inverse_freq = 500000.0 ** (-exponents)
    angles = positions.astype(jnp.float32)[:, None] * inverse_freq[None, :]
    cosine = jnp.cos(angles)[:, None, :]
    sine_part = jnp.sin(angles)[:, None, :]
    front_half = states[..., :half_width]
    back_half = states[..., half_width:]
    return jnp.concatenate(
        [front_half * cosine - back_half * sine_part, back_half * cosine + front_half * sine_part],
        axis=-1,
    )


def per_device(
    queries, key_states, value_states, vertical_blocks, slash_offsets, positions, out_weight
):
    local_tokens = queries.shape[0]
    local_heads = queries.shape[1] // HD
    head_index = lax.axis_index("head")
    ctx_index = lax.axis_index("ctx")
    shared_head = head_index * local_heads // GROUP
    own_keys = lax.dynamic_slice_in_dim(key_states, shared_head * HD, HD, 1)
    own_values = lax.dynamic_slice_in_dim(value_states, shared_head * HD, HD, 1)
    rotated_own = rotate_heads(own_keys.astype(jnp.float32)[:, None, :], positions)[:, 0, :].astype(
        jnp.bfloat16
    )
    all_keys, all_values = (
        lax.all_gather(rotated_own, "ctx", axis=0, tiled=True),
        lax.all_gather(own_values, "ctx", axis=0, tiled=True),
    )
    query_rot = rotate_heads(
        queries.astype(jnp.float32).reshape(local_tokens, local_heads, HD), positions
    ).astype(jnp.bfloat16)
    query_blocks = local_tokens // BLK
    key_count = all_keys.shape[0] // BLK
    block_ids = ctx_index * query_blocks + jnp.arange(query_blocks, dtype=jnp.int32)
    vert_slots = jnp.broadcast_to(
        vertical_blocks[:, None, :], (local_heads, query_blocks, vertical_blocks.shape[1])
    )
    vert_valid = vert_slots <= block_ids[None, :, None]
    slash_slots = block_ids[None, :, None] - slash_offsets[:, None, :]
    repeated = jnp.any(slash_slots[..., None] == vertical_blocks[:, None, None, :], axis=-1)
    slash_valid = (slash_slots >= 0) & jnp.logical_not(repeated)
    slot_blocks = jnp.concatenate([vert_slots, slash_slots], axis=-1)
    slot_valid = jnp.concatenate([vert_valid, slash_valid], axis=-1)
    safe_blocks = jnp.clip(slot_blocks, 0, key_count - 1)
    key_tiles = all_keys.reshape(key_count, BLK, HD)[safe_blocks]
    value_tiles = all_values.reshape(key_count, BLK, HD)[safe_blocks]
    query_tiles = query_rot.reshape(query_blocks, BLK, local_heads, HD).transpose(2, 0, 1, 3)
    scores = jnp.einsum(
        "hqrd,hqskd->hqrsk", query_tiles, key_tiles, preferred_element_type=jnp.float32
    ) / math.sqrt(HD)
    diagonal = (slot_blocks == block_ids[None, :, None])[:, :, None, :, None]
    causal_pairs = (jnp.arange(BLK)[None, :] <= jnp.arange(BLK)[:, None])[None, None, :, None, :]
    allowed = slot_valid[:, :, None, :, None] & (jnp.logical_not(diagonal) | causal_pairs)
    masked = jnp.where(allowed, scores, -1e30)
    row_max = jnp.max(masked, axis=(3, 4), keepdims=True)
    exponentials = jnp.exp(masked - row_max)
    weights = (exponentials / jnp.sum(exponentials, axis=(3, 4), keepdims=True)).astype(
        jnp.bfloat16
    )
    attended = jnp.einsum(
        "hqrsk,hqskd->hqrd", weights, value_tiles, preferred_element_type=jnp.float32
    ).astype(jnp.bfloat16)
    head_out = attended.transpose(1, 2, 0, 3).reshape(local_tokens, local_heads * HD)
    partial_terms = jnp.dot(
        lax.all_gather(head_out, "ctx", axis=0, tiled=True),
        out_weight,
        preferred_element_type=jnp.float32,
    )
    projected = lax.psum_scatter(
        partial_terms.astype(jnp.bfloat16), "head", scatter_dimension=0, tiled=True
    )
    return projected


def solution(mesh):
    placed = (
        P("ctx", "head"),
        P("ctx", None),
        P("ctx", None),
        P("head", None),
        P("head", None),
        P("ctx"),
        P("head", "ctx"),
    )
    return jax.shard_map(
        per_device, mesh=mesh, in_specs=placed, out_specs=P("head", "ctx"), check_vma=False
    )
```

profile of v0, /device:TPU:8, one launch (start us, length us, event | category | flops | bytes accessed | tf_op | source)
XLA Modules:
  0.0 370.9 jit_solution(2328928914875954693)
XLA Ops:
  6.6 1.0 constant_dynamic-slice_fusion.1
  7.6 0.1 copy.56
  7.7 0.7 convert_element_type.25
  8.4 0.3 fusion.14
  8.7 0.6 pad_maximum_fusion
  9.4 1.5 constant_dynamic-slice_fusion
  11.0 0.8 broadcast_subtract_fusion
  11.7 0.7 broadcast_in_dim.15
  12.6 0.7 compare_reduce_fusion
  13.3 0.8 broadcast_compare_fusion
  14.1 0.1 copy.41
  14.2 0.7 broadcast_in_dim.12
  15.0 0.1 copy.42
  15.0 1.1 convert_bitcast_fusion
  16.2 0.2 copy.57
  16.4 0.5 multiply_cosine_fusion
  17.0 0.3 fusion.21
  17.3 1.4 subtract_convert_fusion
  18.7 47.3 %all-gather.9.cloned.1.call-done = bf16[4096,1,128]{0,2,1:T(8,128)(2,1)} async-done(((bf16[256,1,128]{0,2,1:T(8,128)(2,1)}), bf16[4096,1,128]{0,2,1:T(8,128)(2,1)}) %all-gather.9.cloned.1.call-update) | async-done | bytes 1048592 | tf_op jit(solution)/shard_map/all_gather | solution.py:41
  66.0 1.6 copy.53
  67.6 3.0 gather_fusion
  70.7 48.9 %all-gather.5.cloned.1.call-done = bf16[4096,128]{1,0:T(8,128)(2,1)} async-done(((bf16[256,128]{1,0:T(8,128)(2,1)}), bf16[4096,128]{1,0:T(8,128)(2,1)}) %all-gather.5.cloned.1.call-update) | async-done | bytes 1048592 | tf_op jit(solution)/shard_map/all_gather | solution.py:42
  119.6 4.4 %gather_fusion.1 = bf16[128,128,128]{2,1,0:T(8,128)(2,1)} fusion(bf16[32,128,128]{2,1,0:T(8,128)(2,1)} %bitcast.44, s32[1024]{0:T(1024)S(1)} %pad_clamp_fusion), kind=kCustom, calls=%fused_computation.1 | custom fusion | bytes 8389120 | tf_op jit(solution)/shard_map/gather | solution.py:61
  124.0 3.9 %fusion.1 = (f32[8,2,128]{2,1,0:T(2,128)S(1)}, f32[8,2,128,8,128]{2,4,3,1,0:T(8,128)S(1)}) fusion(pred[128,128]{0,1:T(8,128)(4,1)S(1)} %iota_compare_fusion, pred[8,2,8]{2,1,0:T(4,128)(4,1)S(1)} %copy.42, pred[8,2,8]{2,1,0:T(4,128)(4,1)S(1)} %copy.41, bf16[8,2,8,128,128]{4,3,2,1,0:T(8,128)(2,1)} %bitcast.47, bf16[2,128,8,64]{3,1,0,2:T(8,128)(2,1)S(1)} %bitcast.51, ...), kind=kOutput, calls=%fused_computation.7 | convolution fusion | flops 548403200 | bytes 13132032 | tf_op jit(solution)/shard_map/hqrd,hqskd->hqrsk/dot_general | solution.py:63
  127.9 3.0 fusion
  130.9 3.9 %fusion.5 = bf16[2,128,8,128]{3,1,0,2:T(8,128)(2,1)S(1)} fusion(bf16[8,2,8,128,128]{4,3,2,1,0:T(8,128)(2,1)S(1)} %bitcast.46, f32[8,2,128,8,128]{2,4,3,1,0:T(8,128)S(1)} %get-tuple-element.18, f32[8,2,128]{2,1,0:T(2,128)S(1)} %fusion, f32[8,2,128]{2,1,0:T(2,128)S(1)} %get-tuple-element.17, pred[128,128]{0,1:T(8,128)(4,1)S(1)} %iota_compare_fusion, ...), kind=kOutput, calls=%fused_computation.11 | convolution fusion | flops 551813120 | bytes 13140224 | tf_op jit(solution)/shard_map/hqrsk,hqskd->hqrd/dot_general | solution.py:75
  134.8 0.3 copy.49
  135.2 0.9 copy.64
  136.1 0.2 reduce-scatter.2.cloned.1.call-start
  136.3 101.2 %all-gather.7.cloned.1.call-done = bf16[4096,1024]{1,0:T(8,128)(2,1)} async-done(((bf16[256,1024]{1,0:T(8,128)(2,1)}), bf16[4096,1024]{1,0:T(8,128)(2,1)}) %all-gather.7.cloned.1.call-update) | async-done | bytes 8388624 | tf_op jit(solution)/shard_map/all_gather | solution.py:80
  237.5 14.5 %convolution_convert_fusion = bf16[4096,1024]{1,0:T(8,128)(2,1)} fusion(bf16[4096,1024]{1,0:T(8,128)(2,1)} %all-gather.7.cloned.1.call-done, bf16[1024,1024]{1,0:T(8,128)(2,1)S(1)} %copy-done), kind=kOutput, calls=%fused_computation.5 | convolution fusion | flops 8594128896 | bytes 18874368 | tf_op jit(solution)/shard_map/dot_general | solution.py:79
  252.0 112.3 %reduce-scatter.2.cloned.1.call-done = bf16[256,1024]{1,0:T(8,128)(2,1)} async-done(((bf16[4096,1024]{1,0:T(8,128)(2,1)}), bf16[256,1024]{1,0:T(8,128)(2,1)}) %reduce-scatter.2.cloned.1.call-update) | async-done | bytes 524304 | tf_op jit(solution)/shard_map/reduce_scatter | solution.py:84
  (25 shorter events, 0.5 us)
Async XLA Ops:
  6.5 230.9 %copy-start = (bf16[1024,1024]{1,0:T(8,128)(2,1)S(1)}, bf16[1024,1024]{1,0:T(8,128)(2,1)}, u32[]{:S(2)}) copy-start(bf16[1024,1024]{1,0:T(8,128)(2,1)} %param.13) | copy-start | bytes 6291460
  6.5 59.4 %all-gather.9.cloned.1.call-start = ((), (), s32[]{:S(2)}) async-start(), calls=%async_computation.4 | async-start | bytes 1114112 | tf_op jit(solution)/shard_map/all_gather | solution.py:41
  9.4 110.2 %all-gather.5.cloned.1.call-start = ((), (), s32[]{:S(2)}) async-start(), calls=%async_computation.1 | async-start | bytes 1114112 | tf_op jit(solution)/shard_map/all_gather | solution.py:42
  10.9 226.6 %all-gather.7.cloned.1.call-start = ((), (), s32[]{:S(2)}) async-start(), calls=%async_computation.2 | async-start | bytes 8912896 | tf_op jit(solution)/shard_map/all_gather | solution.py:80
  119.6 4.4 %copy-start.2 = (bf16[256,8,64]{2,0,1:T(8,128)(2,1)S(1)}, bf16[256,8,64]{2,0,1:T(8,128)(2,1)}, u32[]{:S(2)}) copy-start(bf16[256,8,64]{2,0,1:T(8,128)(2,1)} %get-tuple-element.5) | copy-start | bytes 786436
  119.6 4.4 %copy-start.3 = (bf16[256,8,64]{2,0,1:T(8,128)(2,1)S(1)}, bf16[256,8,64]{2,0,1:T(8,128)(2,1)}, u32[]{:S(2)}) copy-start(bf16[256,8,64]{2,0,1:T(8,128)(2,1)} %get-tuple-element.6) | copy-start | bytes 786436
  127.9 3.0 copy-start.1
  136.1 228.3 %reduce-scatter.2.cloned.1.call-start = ((), (), s32[]{:S(2)}) async-start(), calls=%async_computation.3 | async-start | bytes 8912896 | tf_op jit(solution)/shard_map/reduce_scatter | solution.py:84
Sparse Core Ops, SparseCore 0:
  9.8 56.1 all-gather.8
  68.4 51.1 all-gather.4
  136.2 101.2 all-gather.6
  252.1 112.1 reduce-scatter.1
where the time goes:
time: 371 us
  waiting for transfers between devices  310 us (84%)
  matrix products  22.3 us (6%)
  local copies, waits for them, and re-layouts  15.1 us (4%)
  between operations  13.3 us (4%)
  other arithmetic  10.1 us (3%)
    reduce_scatter x1, waiting for transfers between devices, per_device(): lax.psum_scatter(partial_terms.astype(jnp.bfloat16), 'head', scatter_dime...  112 us
    all_gather x1, waiting for transfers between devices, per_device(): lax.all_gather(head_out, 'ctx', axis=0, tiled=True)  101 us
    all_gather x1, waiting for transfers between devices, per_device(): lax.all_gather(own_values, 'ctx', axis=0, tiled=True)  48.9 us
    all_gather x1, waiting for transfers between devices, per_device(): lax.all_gather(rotated_own, 'ctx', axis=0, tiled=True)  47.3 us
    dot_general x1, matrix products, per_device(): jnp.dot(lax.all_gather(head_out, 'ctx', axis=0, tiled=True), out_weight,...  14.5 us
  transfers between devices with their start and end apart: 4, of which 4 were waited for; matrix products, arithmetic and copies ran while one was open for 4% of the time, Pallas kernels for 0%

commit v1 on v0

--- a/solution.py
+++ b/solution.py
@@ -77,7 +77,9 @@
     ).astype(jnp.bfloat16)
     head_out = attended.transpose(1, 2, 0, 3).reshape(local_tokens, local_heads * HD)
     partial_terms = jnp.dot(
-        lax.all_gather(head_out, "ctx", axis=0, tiled=True),
+        jnp.concatenate(
+            lax.all_to_all(jnp.stack([head_out] * lax.axis_size("ctx")), "ctx", 0, 0), axis=0
+        ),
         out_weight,
         preferred_element_type=jnp.float32,
     )

time: 371 us -> 442 us (1.19)
  blocking collectives: 0 us -> 148 us
  waiting for transfers between devices: 310 us -> 237 us
    all_to_all x0 -> x1, blocking collectives: none -> 148 us  [per_device(): lax.all_to_all(jnp.stack([head_out] * lax.axis_size('ctx')), 'ctx', 0, 0)]
    all_gather x1 -> x0, waiting for transfers between devices: 101 us -> none  [per_device(): lax.all_gather(head_out, 'ctx', axis=0, tiled=True)]
    reduce_scatter x1, waiting for transfers between devices: 112 us -> 141 us  [per_device(): lax.psum_scatter(partial_terms.astype(jnp.bfloat16), 'head', scatter_dime...]
  transfers between devices with their start and end apart: 4 -> 3, of which waited for: 4 -> 3; matrix products, arithmetic and copies ran while one was open for 4% -> 3% of each run, Pallas kernels for 0% -> 0%
where the time goes in v1:
time: 442 us
  waiting for transfers between devices  237 us (54%)
  blocking collectives  148 us (33%)
  matrix products  18.6 us (4%)
  local copies, waits for them, and re-layouts  15.4 us (3%)
  between operations  13.3 us (3%)
  other arithmetic  10.1 us (2%)
    all_to_all x1, blocking collectives, per_device(): lax.all_to_all(jnp.stack([head_out] * lax.axis_size('ctx')), 'ctx', 0, 0)  148 us
    reduce_scatter x1, waiting for transfers between devices, per_device(): lax.psum_scatter(partial_terms.astype(jnp.bfloat16), 'head', scatter_dime...  141 us
    all_gather x1, waiting for transfers between devices, per_device(): lax.all_gather(own_values, 'ctx', axis=0, tiled=True)  49 us
    all_gather x1, waiting for transfers between devices, per_device(): lax.all_gather(rotated_own, 'ctx', axis=0, tiled=True)  47.3 us
    dot_general x1, matrix products, per_device(): jnp.dot(jnp.concatenate(lax.all_to_all(jnp.stack([head_out] * lax.axis_si...  10.8 us
  transfers between devices with their start and end apart: 3, of which 3 were waited for; matrix products, arithmetic and copies ran while one was open for 3% of the time, Pallas kernels for 0%

profile of v1, /device:TPU:8, one launch (start us, length us, event | category | flops | bytes accessed | tf_op | source)
XLA Modules:
  0.0 441.9 jit_solution(9192286568672439561)
XLA Ops:
  6.6 1.0 constant_dynamic-slice_fusion.1
  7.6 0.1 copy.56
  7.7 0.7 convert_element_type.25
  8.4 0.3 fusion.14
  8.7 0.6 pad_maximum_fusion
  9.4 1.5 constant_dynamic-slice_fusion
  11.0 0.8 broadcast_subtract_fusion
  11.7 0.7 broadcast_in_dim.15
  12.5 0.1 reshape.191
  12.6 0.7 compare_reduce_fusion
  13.3 0.8 broadcast_compare_fusion
  14.1 0.1 copy.41
  14.2 0.7 broadcast_in_dim.12
  15.0 0.1 copy.42
  15.1 1.1 convert_bitcast_fusion
  16.2 0.2 copy.57
  16.4 0.5 multiply_cosine_fusion
  17.0 0.3 fusion.21
  17.3 1.4 subtract_convert_fusion
  18.7 47.3 %all-gather.6.cloned.1.call-done = bf16[4096,1,128]{0,2,1:T(8,128)(2,1)} async-done(((bf16[256,1,128]{0,2,1:T(8,128)(2,1)}), bf16[4096,1,128]{0,2,1:T(8,128)(2,1)}) %all-gather.6.cloned.1.call-update) | async-done | bytes 1048592 | tf_op jit(solution)/shard_map/all_gather | solution.py:41
  66.0 1.6 copy.53
  67.6 3.0 gather_fusion
  70.6 49.0 %all-gather.4.cloned.1.call-done = bf16[4096,128]{1,0:T(8,128)(2,1)} async-done(((bf16[256,128]{1,0:T(8,128)(2,1)}), bf16[4096,128]{1,0:T(8,128)(2,1)}) %all-gather.4.cloned.1.call-update) | async-done | bytes 1048592 | tf_op jit(solution)/shard_map/all_gather | solution.py:42
  119.6 4.4 gather_fusion.1
  124.0 3.9 fusion.1
  127.9 3.0 fusion
  130.9 3.8 fusion.5
  134.8 0.3 copy.49
  135.2 1.1 stack.3
  136.3 147.6 %all_to_all.5 = bf16[16,256,1024]{2,1,0:T(8,128)(2,1)S(1)} all-to-all(bf16[16,256,1024]{2,1,0:T(8,128)(2,1)S(1)} %stack.3), channel_id=1, replica_groups=mesh['ctx'=16,'head'=16] {'ctx'}, dimensions={0} | all-to-all | bytes 16777216 | tf_op jit(solution)/shard_map/all_to_all | solution.py:81
  284.0 10.8 %convolution_convert_fusion = bf16[4096,1024]{1,0:T(8,128)(2,1)} fusion(bf16[4096,1024]{1,0:T(8,128)(2,1)S(1)} %bitcast.47, bf16[1024,1024]{1,0:T(8,128)(2,1)S(1)} %copy-done), kind=kOutput, calls=%fused_computation.5 | convolution fusion | flops 8594128896 | bytes 18874368 | tf_op jit(solution)/shard_map/dot_general | solution.py:79
  294.8 140.6 %reduce-scatter.2.cloned.1.call-done = bf16[256,1024]{1,0:T(8,128)(2,1)} async-done(((bf16[4096,1024]{1,0:T(8,128)(2,1)}), bf16[256,1024]{1,0:T(8,128)(2,1)}) %reduce-scatter.2.cloned.1.call-update) | async-done | bytes 524304 | tf_op jit(solution)/shard_map/reduce_scatter | solution.py:86
  (24 shorter events, 0.5 us)
Async XLA Ops:
  6.5 277.4 %copy-start = (bf16[1024,1024]{1,0:T(8,128)(2,1)S(1)}, bf16[1024,1024]{1,0:T(8,128)(2,1)}, u32[]{:S(2)}) copy-start(bf16[1024,1024]{1,0:T(8,128)(2,1)} %param.13) | copy-start | bytes 6291460
  6.5 59.4 %all-gather.6.cloned.1.call-start = ((), (), s32[]{:S(2)}) async-start(), calls=%async_computation.4 | async-start | bytes 1114112 | tf_op jit(solution)/shard_map/all_gather | solution.py:41
  9.4 110.2 %all-gather.4.cloned.1.call-start = ((), (), s32[]{:S(2)}) async-start(), calls=%async_computation.2 | async-start | bytes 1114112 | tf_op jit(solution)/shard_map/all_gather | solution.py:42
  10.9 424.5 %reduce-scatter.2.cloned.1.call-start = ((), (), s32[]{:S(2)}) async-start(), calls=%async_computation.3 | async-start | bytes 8912896 | tf_op jit(solution)/shard_map/reduce_scatter | solution.py:86
  119.6 4.4 copy-start.2
  119.6 4.4 copy-start.3
  127.9 3.1 copy-start.1
Sparse Core Ops, SparseCore 0:
  9.8 56.1 all-gather.5
  68.4 51.1 all-gather.3
  294.9 140.4 reduce-scatter.1
